TPU v7x, 512 devices: a whole 4x4x16 slice. The times are simulated.
512 devices in a mesh: wide: 128 (over z, x, core), narrow: 4 (over y).
Axes of the slice: x: 4, y: 4, z: 16, core: 2. Of those that a mesh axis runs over, the one named last changes fastest.
Arguments:
- tokens_in: bfloat16 [16384, 2560], P('wide', 'narrow'), may hold values from -6 to 6
- norm_gain: bfloat16 [2560], replicated, may hold values from 0.099609375 to 1.8984375
- query_weight: bfloat16 [2560, 2560], P('wide', 'narrow'), may hold values from -0.25 to 0.25
- key_weight: bfloat16 [2560, 640], P('wide', 'narrow'), may hold values from -0.125 to 0.125
- value_weight: bfloat16 [2560, 640], P('wide', 'narrow'), may hold values from -0.5 to 0.5
- out_weight: bfloat16 [2560, 2560], P('wide', 'narrow'), may hold values from -0.125 to 0.125
- cache_keys: bfloat16 [640, 131072], P('narrow', 'wide'), may hold values from -64 to 64
- cache_values: bfloat16 [640, 131072], P('narrow', 'wide'), may hold values from -24 to 24
- cached_len: int32 [32], replicated, may hold values from 1 to 4096, as said below
- append_slot: int32 [32], replicated, may hold values from 0 to 4095
- shard_owner: int32 [32], replicated, may hold values from 0 to 3
Outputs:
- attention_update: bfloat16 [16384, 2560], P('wide', 'narrow')
- appended_keys: bfloat16 [640, 131072], P('narrow', 'wide')
- appended_values: bfloat16 [640, 131072], P('narrow', 'wide')
Inputs may be any that keep to these rules, and one draw needn't show every extreme that they name: `cached_len`: each request's number of cached keys; some request holds 4096.
All inputs are finite; a program needn't handle non-finite values.
Results may differ from a plain program's by a relative error of at most 0.012.
The roundings to bfloat16 on the way count: a program that leaves them out, or rounds other values in their place, can miss the bound.
Values may be sent and summed in bfloat16 or wider, within the bound.
A program may use at most 64 MiB of HBM per device.

v0:
```python
import math
import jax
import jax.numpy as jnp
from jax import lax
from jax.sharding import PartitionSpec as P

HEAD_DIM = 80
WIN = 4096
GROUP_BITS = 2
GROUP = 4
EPSILON = 1e-05
ROPE_BASE = 10000.0
LOWEST = -1e30


def from_partner(block, axis, bit):
    count = lax.axis_size(axis)
    route = []
    for low in range(count):
        high = low | 1 << bit
        if high != low and high < count:
            route += [(low, high), (high, low)]
    return lax.ppermute(block, axis, route)


def rms_normed(rows_in, gain):
    values = rows_in.astype(jnp.float32)
    scaling = lax.rsqrt(jnp.mean(values * values, axis=-1, keepdims=True) + EPSILON)
    return (values * scaling * gain.astype(jnp.float32)).astype(jnp.bfloat16)


def rotate(values, positions):
    half_dim = values.shape[-1] // 2
    inverse = ROPE_BASE ** (-(jnp.arange(half_dim, dtype=jnp.float32) * (2.0 / values.shape[-1])))
    angles = positions.astype(jnp.float32)[:, None] * inverse[None, :]
    cos_part = jnp.cos(angles)[:, None, :]
    sin_part = jnp.sin(angles)[:, None, :]
    lower = values[..., :half_dim]
    higher = values[..., half_dim:]
    return jnp.concatenate(
        [lower * cos_part - higher * sin_part, higher * cos_part + lower * sin_part], axis=-1
    )


def ordered(mine, other, upper, along):
    first_half = jnp.where(upper, other, mine)
    second_half = jnp.where(upper, mine, other)
    return jnp.concatenate([first_half, second_half], axis=along)


def empty_state(row_count, groups, repeats):
    return (
        jnp.zeros((row_count, groups, repeats, HEAD_DIM), jnp.float32),
        jnp.full((row_count, groups, repeats), LOWEST, jnp.float32),
        jnp.zeros((row_count, groups, repeats), jnp.float32),
    )


def fold_keys(state, queries, query_pos, keys, values, key_pos, key_ok, widest):
    key_count = keys.shape[1]
    groups = queries.shape[1]
    block = math.gcd(key_count, widest)
    keys_split = keys.reshape(groups, HEAD_DIM, key_count)
    values_split = values.reshape(groups, HEAD_DIM, key_count)
    scale = HEAD_DIM ** (-0.5)

    def step(index, carry):
        accum, top_old, sum_old = carry
        start = index * block
        block_keys = lax.dynamic_slice_in_dim(keys_split, start, block, 2)
        block_values = lax.dynamic_slice_in_dim(values_split, start, block, 2)
        block_pos = lax.dynamic_slice_in_dim(key_pos, start, block, 0)
        block_ok = lax.dynamic_slice_in_dim(key_ok, start, block, 0)
        scores = (
            jnp.einsum("tgrd,gdk->tgrk", queries, block_keys, preferred_element_type=jnp.float32)
            * scale
        )
        allowed = (
            block_ok[None, :]
            & (block_pos[None, :] <= query_pos[:, None])
            & (query_pos[:, None] - block_pos[None, :] < WIN)
        )
        allowed = allowed[:, None, None, :]
        top_new = jnp.maximum(top_old, jnp.max(jnp.where(allowed, scores, LOWEST), axis=-1))
        weights = jnp.where(allowed, jnp.exp(scores - top_new[..., None]), 0.0)
        rescale = jnp.exp(top_old - top_new)
        sum_new = sum_old * rescale + jnp.sum(weights, axis=-1)
        mixed = jnp.einsum(
            "tgrk,gdk->tgrd",
            weights.astype(jnp.bfloat16),
            block_values,
            preferred_element_type=jnp.float32,
        )
        return (accum * rescale[..., None] + mixed, top_new, sum_new)

    return lax.fori_loop(0, key_count // block, step, state)


def shards(
    tokens_in,
    norm_gain,
    query_weight,
    key_weight,
    value_weight,
    out_weight,
    cache_keys,
    cache_values,
    cached_len,
    append_slot,
    shard_owner,
):
    whole = lax.all_gather(tokens_in, "narrow", axis=1, tiled=True)
    normed = rms_normed(whole, norm_gain)
    tok_rows = whole.shape[0]
    query_width = query_weight.shape[1]
    kv_width = key_weight.shape[1]
    local_heads = query_width // HEAD_DIM
    local_groups = kv_width // HEAD_DIM
    repeats = local_heads // local_groups
    columns = normed
    query_sum = jnp.dot(
        columns,
        lax.all_gather(query_weight, "wide", axis=0, tiled=True),
        preferred_element_type=jnp.float32,
    )
    key_sum = jnp.dot(
        columns,
        lax.all_gather(key_weight, "wide", axis=0, tiled=True),
        preferred_element_type=jnp.float32,
    )
    value_sum = jnp.dot(
        columns,
        lax.all_gather(value_weight, "wide", axis=0, tiled=True),
        preferred_element_type=jnp.float32,
    )
    position = lax.axis_index("wide")
    request = position // GROUP
    place = position % GROUP
    length = cached_len[request]
    offset = append_slot[request]
    owner = shard_owner[request]
    query_pos = length + place * tok_rows + jnp.arange(tok_rows, dtype=jnp.int32)
    queries = rotate(query_sum.reshape(tok_rows, local_heads, HEAD_DIM), query_pos).astype(
        jnp.bfloat16
    )
    queries = queries.reshape(tok_rows, local_groups, repeats, HEAD_DIM)
    new_keys = (
        rotate(key_sum.reshape(tok_rows, local_groups, HEAD_DIM), query_pos)
        .astype(jnp.bfloat16)
        .reshape(tok_rows, kv_width)
    )
    new_values = value_sum.astype(jnp.bfloat16)
    shard_rows = cache_keys.shape[1]
    within = jnp.arange(shard_rows, dtype=jnp.int32)
    cycle_mine = (place - owner) % GROUP * shard_rows + within
    old_keys, old_values = (cache_keys, cache_values)
    for bit in range(GROUP_BITS):
        upper = place // 2**bit % 2 == 1
        other_keys, other_values, other_old_keys, other_old_values = from_partner(
            (new_keys, new_values, old_keys, old_values), "wide", bit
        )
        new_keys = ordered(new_keys, other_keys, upper, 0)
        new_values = ordered(new_values, other_values, upper, 0)
        old_keys = ordered(old_keys, other_old_keys, upper, 1)
        old_values = ordered(old_values, other_old_values, upper, 1)
    slot_index = jnp.arange(old_keys.shape[1], dtype=jnp.int32)
    cycle = (slot_index // shard_rows - owner) % GROUP * shard_rows + slot_index % shard_rows
    cached_pos = (cycle - offset + length) % WIN
    state = fold_keys(
        empty_state(tok_rows, local_groups, repeats),
        queries,
        query_pos,
        old_keys,
        old_values,
        cached_pos,
        cached_pos < length,
        512,
    )
    key_cols = new_keys.T
    value_cols = new_values.T
    new_count = key_cols.shape[1]
    new_pos = length + jnp.arange(new_count, dtype=jnp.int32)
    state = fold_keys(
        state,
        queries,
        query_pos,
        key_cols,
        value_cols,
        new_pos,
        jnp.ones((new_count,), dtype=bool),
        512,
    )
    accum, top_score, total = state
    attended = (accum / total[..., None]).astype(jnp.bfloat16).reshape(tok_rows, query_width)
    all_heads = lax.all_gather(attended, "narrow", axis=1, tiled=True)
    columns = all_heads
    update = jnp.dot(
        columns,
        lax.all_gather(out_weight, "wide", axis=0, tiled=True),
        preferred_element_type=jnp.float32,
    ).astype(jnp.bfloat16)
    new_index = (cycle_mine - offset) % WIN
    written = new_index < new_count
    take_rows = jnp.minimum(new_index, new_count - 1)
    put_keys = jnp.where(written[None, :], jnp.take(key_cols, take_rows, axis=1), cache_keys)
    put_values = jnp.where(written[None, :], jnp.take(value_cols, take_rows, axis=1), cache_values)
    return (update, put_keys, put_values)


def solution(mesh):
    in_specs = (
        P("wide", "narrow"),
        P(),
        P("wide", "narrow"),
        P("wide", "narrow"),
        P("wide", "narrow"),
        P("wide", "narrow"),
        P("narrow", "wide"),
        P("narrow", "wide"),
        P(),
        P(),
        P(),
    )
    out_specs = (P("wide", "narrow"), P("narrow", "wide"), P("narrow", "wide"))
    return jax.shard_map(shards, mesh=mesh, in_specs=in_specs, out_specs=out_specs, check_vma=False)
```

profile of v0, /device:TPU:1, one launch (start us, length us, event | category | flops | bytes accessed | tf_op | source)
XLA Modules:
  0.0 399.1 jit_solution(11105308332598685223)
XLA Ops:
  8.0 109.3 %all-gather.2 = bf16[128,20,160]{2,1,0:T(8,128)(2,1)S(1)} all-gather(bf16[1,20,160]{2,1,0:T(8,128)(2,1)} %bitcast.135), channel_id=1, replica_groups=mesh['wide'=128,'narrow'=4] {'wide'}, dimensions={0}, use_global_device_ids=true | all-gather | bytes 825600 | tf_op jit(solution)/shard_map/all_gather | solution.py:133
  117.9 12.4 %all_gather.18 = bf16[128,2560]{1,0:T(8,128)(2,1)S(1)} all-gather(bf16[128,640]{1,0:T(8,128)(2,1)} %param.15), channel_id=1, replica_groups=mesh['wide'=128,'narrow'=4] {'narrow'}, dimensions={1}, use_global_device_ids=true | all-gather | bytes 819200 | tf_op jit(solution)/shard_map/all_gather | solution.py:112
  131.8 4.1 %collective-permute-start.6 = (bf16[128,160]{0,1:T(8,128)(2,1)}, bf16[128,160]{0,1:T(8,128)(2,1)}, u32[]{:S(2)}, u32[]{:S(2)}) collective-permute-start(bf16[128,160]{0,1:T(8,128)(2,1)} %convolution_convert_fusion.1), channel_id=1, source_target_pairs={{0,4},{4,0},{8,12},{12,8},{16,20},{20,16},{24,28},{28,24},{32,36},... | collective-permute-start | bytes 122888 | tf_op jit(solution)/shard_map/ppermute | solution.py:23
  135.9 100.1 %all-gather.1 = bf16[128,20,160]{2,1,0:T(8,128)(2,1)S(1)} all-gather(bf16[1,20,160]{2,1,0:T(8,128)(2,1)} %bitcast.136), channel_id=1, replica_groups=mesh['wide'=128,'narrow'=4] {'wide'}, dimensions={0}, use_global_device_ids=true | all-gather | bytes 825600 | tf_op jit(solution)/shard_map/all_gather | solution.py:128
  239.4 2.1 collective-permute-start.4
  241.5 2.3 collective-permute-start.2
  243.8 2.3 collective-permute-start
  248.0 2.5 broadcast_compare_fusion
  250.5 2.5 add_select_fusion
  259.2 1.9 collective-permute-start.7
  261.2 3.4 collective-permute-start.5
  270.1 2.8 collective-permute-start.1
  274.7 5.3 %gather_fusion.1 = bf16[1024,160]{1,0:T(8,128)(2,1)} fusion(bf16[160,512]{0,1:T(8,128)(2,1)S(1)} %copy.40, s32[1024]{0:T(1024)} %fusion.54), kind=kCustom, calls=%fused_computation.1.clone | custom fusion | bytes 659456 | tf_op jit(solution)/shard_map/jit(_take)/gather | solution.py:206
  280.0 5.3 %gather_fusion = bf16[1024,160]{1,0:T(8,128)(2,1)} fusion(bf16[160,512]{0,1:T(8,128)(2,1)S(1)} %copy.38, s32[1024]{0:T(1024)} %fusion.54), kind=kCustom, calls=%fused_computation.clone | custom fusion | bytes 659456 | tf_op jit(solution)/shard_map/jit(_take)/gather | solution.py:205
  285.3 2.5 bitcast_select_fusion.2
  287.8 1.9 copy.42
  290.7 2.4 collective-permute-start.3
  295.8 11.1 %collective-permute-done.3 = bf16[160,2048]{1,0:T(8,128)(2,1)S(1)} collective-permute-done((bf16[160,2048]{1,0:T(8,128)(2,1)S(1)}, bf16[160,2048]{1,0:T(8,128)(2,1)S(1)}, u32[]{:S(2)}, u32[]{:S(2)}) %collective-permute-start.3) | collective-permute-done | bytes 655392 | tf_op jit(solution)/shard_map/ppermute | solution.py:23
  308.4 6.1 %reshape.265 = bf16[2560,640]{1,0:T(8,128)(2,1)} reshape(bf16[128,20,640]{2,1,0:T(8,128)(2,1)} %all-gather.7.cloned.1.call-done) | data formatting | bytes 6553600
  314.5 3.4 fusion.64
  318.1 41.1 %while.5 = (s32[]{:T(128)}, f32[128,2,4,80]{0,3,2,1:T(8,128)S(1)}, f32[128,2,4]{0,2,1:T(4,128)S(1)}, f32[128,2,4]{0,2,1:T(4,128)S(1)}, pred[4096]{0:T(1024)(128)...) while((s32[]{:T(128)}, f32[128,2,4,80]{0,3,2,1:T(8,128)S(1)}, ...), condition=%wide.region_4.5_spmd.clone, body=%wide.region_1.4_spmd.clone.sunk | while | flops 174118016 | bytes 7774939 | solution.py:96
  321.7 1.5 fusion.89
  326.8 1.5 fusion.89
  331.9 1.5 fusion.89
  337.0 1.5 fusion.89
  342.1 1.5 fusion.89
  347.3 1.5 fusion.89
  357.6 1.5 fusion.89
  360.7 11.0 %all_gather.22 = bf16[128,2560]{0,1:T(8,128)(2,1)S(1)} all-gather(bf16[128,640]{0,1:T(8,128)(2,1)S(1)} %bitcast.129), channel_id=1, replica_groups=mesh['wide'=128,'narrow'=4] {'narrow'}, dimensions={1}, use_global_device_ids=true | all-gather | bytes 819200 | tf_op jit(solution)/shard_map/all_gather | solution.py:195
  371.7 11.2 %all-gather.9.cloned.1.call-done = bf16[128,20,640]{2,1,0:T(8,128)(2,1)} async-done(((bf16[1,20,640]{2,1,0:T(8,128)(2,1)}), bf16[128,20,640]{2,1,0:T(8,128)(2,1)}) %all-gather.9.cloned.1.call-update) | async-done | bytes 3276816 | tf_op jit(solution)/shard_map/all_gather | solution.py:199
  382.9 6.1 %reshape.271 = bf16[2560,640]{1,0:T(8,128)(2,1)} reshape(bf16[128,20,640]{2,1,0:T(8,128)(2,1)} %all-gather.9.cloned.1.call-done) | data formatting | bytes 6553600
  389.0 3.3 convolution_convert_fusion
  (166 shorter events, 57.0 us)
Async XLA Ops:
  7.2 301.2 %all-gather.7.cloned.1.call-start = ((), (), s32[]{:S(2)}) async-start(), calls=%async_computation | async-start | bytes 3962880 | tf_op jit(solution)/shard_map/all_gather | solution.py:123
  7.9 375.0 %all-gather.9.cloned.1.call-start = ((), (), s32[]{:S(2)}) async-start(), calls=%async_computation.1 | async-start | bytes 3962880 | tf_op jit(solution)/shard_map/all_gather | solution.py:199
  7.9 109.9 %copy-start.10 = (bf16[2560]{0:T(1024)(128)(2,1)S(1)}, bf16[2560]{0:T(1024)(128)(2,1)}, u32[]{:S(2)}) copy-start(bf16[2560]{0:T(1024)(128)(2,1)} %param.16) | copy-start | bytes 15364
  130.5 108.2 %copy-start.11 = (f32[128]{0:T(128)}, f32[128]{0:T(128)S(1)}, u32[]{:S(2)}) copy-start(f32[128]{0:T(128)S(1)} %add_rsqrt_fusion) | copy-start | bytes 1540
  131.8 126.6 %collective-permute-start.6 = (bf16[128,160]{0,1:T(8,128)(2,1)}, bf16[128,160]{0,1:T(8,128)(2,1)}, u32[]{:S(2)}, u32[]{:S(2)}) collective-permute-start(bf16[128,160]{0,1:T(8,128)(2,1)} %convolution_convert_fusion.1), channel_id=1, source_target_pairs={{0,4},{4,0},{8,12},{12,8},{16,20},{20,16},{24,28},{28,24},{32,36},... | collective-permute-start | bytes 122888 | tf_op jit(solution)/shard_map/ppermute | solution.py:23
  236.6 4.9 %copy-start = (bf16[160,1024]{1,0:T(8,128)(2,1)S(1)}, bf16[160,1024]{1,0:T(8,128)(2,1)}, u32[]{:S(2)}) copy-start(bf16[160,1024]{1,0:T(8,128)(2,1)} %param.22) | copy-start | bytes 983044
  236.6 10.1 %copy-start.13 = (s32[32]{0:T(128)S(1)}, s32[32]{0:T(128)}, u32[]{:S(2)}) copy-start(s32[32]{0:T(128)} %param.24) | copy-start | bytes 388
  236.6 10.8 %copy-start.14 = (s32[32]{0:T(128)S(1)}, s32[32]{0:T(128)}, u32[]{:S(2)}) copy-start(s32[32]{0:T(128)} %param.25) | copy-start | bytes 388
  238.8 19.6 %copy-start.4 = (f32[128,40]{0,1:T(8,128)}, f32[128,40]{0,1:T(8,128)S(1)}, u32[]{:S(2)}) copy-start(f32[128,40]{0,1:T(8,128)S(1)} %get-tuple-element.305) | copy-start | bytes 61444
  238.8 19.6 %copy-start.6 = (f32[128,40]{0,1:T(8,128)}, f32[128,40]{0,1:T(8,128)S(1)}, u32[]{:S(2)}) copy-start(f32[128,40]{0,1:T(8,128)S(1)} %get-tuple-element.306) | copy-start | bytes 61444
  239.4 18.9 %collective-permute-start.4 = (bf16[128,160]{0,1:T(8,128)(2,1)S(1)}, bf16[128,160]{0,1:T(8,128)(2,1)S(1)}, u32[]{:S(2)}, u32[]{:S(2)}) collective-permute-start(bf16[128,160]{0,1:T(8,128)(2,1)S(1)} %bitcast.127), channel_id=1, source_target_pairs={{0,4},{4,0},{8,12},{12,8},{16,20},{20,16},{24,28},{28,24},{32,36},... | collective-permute-start | bytes 122888 | tf_op jit(solution)/shard_map/ppermute | solution.py:23
  241.5 25.5 %collective-permute-start.2 = (bf16[160,1024]{1,0:T(8,128)(2,1)S(1)}, bf16[160,1024]{1,0:T(8,128)(2,1)S(1)}, u32[]{:S(2)}, u32[]{:S(2)}) collective-permute-start(bf16[160,1024]{1,0:T(8,128)(2,1)S(1)} %copy-done), channel_id=1, source_target_pairs={{0,4},{4,0},{8,12},{12,8},{16,20},{20,16},{24,28},{28,24},{32,36},... | collective-permute-start | bytes 983048 | tf_op jit(solution)/shard_map/ppermute | solution.py:23
  243.8 24.0 %collective-permute-start = (bf16[160,1024]{1,0:T(8,128)(2,1)}, bf16[160,1024]{1,0:T(8,128)(2,1)}, u32[]{:S(2)}, u32[]{:S(2)}) collective-permute-start(bf16[160,1024]{1,0:T(8,128)(2,1)} %param.21), channel_id=1, source_target_pairs={{0,4},{4,0},{8,12},{12,8},{16,20},{20,16},{24,28},{28,24},{32,36},... | collective-permute-start | bytes 983048 | tf_op jit(solution)/shard_map/ppermute | solution.py:23
  259.2 5.7 %collective-permute-start.7 = (bf16[256,160]{0,1:T(8,128)(2,1)S(1)}, bf16[256,160]{0,1:T(8,128)(2,1)S(1)}, u32[]{:S(2)}, u32[]{:S(2)}) collective-permute-start(bf16[256,160]{0,1:T(8,128)(2,1)S(1)} %pad_maximum_fusion.8), channel_id=1, source_target_pairs={{0,8},{8,0},{4,12},{12,4},{16,24},{24,16},{20,28},{28,20},{32,40},... | collective-permute-start | bytes 245768 | tf_op jit(solution)/shard_map/ppermute | solution.py:23
  261.2 5.8 %collective-permute-start.5 = (bf16[256,160]{0,1:T(8,128)(2,1)S(1)}, bf16[256,160]{0,1:T(8,128)(2,1)S(1)}, u32[]{:S(2)}, u32[]{:S(2)}) collective-permute-start(bf16[256,160]{0,1:T(8,128)(2,1)S(1)} %pad_maximum_fusion.7), channel_id=1, source_target_pairs={{0,8},{8,0},{4,12},{12,4},{16,24},{24,16},{20,28},{28,20},{32,40},... | collective-permute-start | bytes 245768 | tf_op jit(solution)/shard_map/ppermute | solution.py:23
  267.0 0.7 copy-start.3
  270.1 23.1 %collective-permute-start.1 = (bf16[160,2048]{1,0:T(8,128)(2,1)}, bf16[160,2048]{1,0:T(8,128)(2,1)}, u32[]{:S(2)}, u32[]{:S(2)}) collective-permute-start(bf16[160,2048]{1,0:T(8,128)(2,1)} %pad_maximum_fusion.2), channel_id=1, source_target_pairs={{0,8},{8,0},{4,12},{12,4},{16,24},{24,16},{20,28},{28,20},{32,40},... | collective-permute-start | bytes 1966088 | tf_op jit(solution)/shard_map/ppermute | solution.py:23
  290.7 16.2 %collective-permute-start.3 = (bf16[160,2048]{1,0:T(8,128)(2,1)S(1)}, bf16[160,2048]{1,0:T(8,128)(2,1)S(1)}, u32[]{:S(2)}, u32[]{:S(2)}) collective-permute-start(bf16[160,2048]{1,0:T(8,128)(2,1)S(1)} %pad_maximum_fusion.3), channel_id=1, source_target_pairs={{0,8},{8,0},{4,12},{12,4},{16,24},{24,16},{20,28},{28,20},{32,40},... | collective-permute-start | bytes 1966088 | tf_op jit(solution)/shard_map/ppermute | solution.py:23
  308.4 6.1 %copy-start.12 = (f32[128]{0:T(128)S(1)}, f32[128]{0:T(128)}, u32[]{:S(2)}) copy-start(f32[128]{0:T(128)} %copy-done.11) | copy-start | bytes 1540
  314.5 3.4 copy-start.5
  314.5 3.4 copy-start.7
  314.5 3.5 copy-start.9
  314.5 3.5 copy-start.15
  318.0 41.1 %copy-start.1 = (bf16[512,160]{0,1:T(8,128)(2,1)S(1)}, bf16[512,160]{0,1:T(8,128)(2,1)}, u32[]{:S(2)}) copy-start(bf16[512,160]{0,1:T(8,128)(2,1)} %get-tuple-element.292) | copy-start | bytes 491524
  318.0 41.1 %copy-start.2 = (pred[128,512]{0,1:T(8,128)(4,1)S(1)}, pred[128,512]{0,1:T(8,128)(4,1)}, u32[]{:S(2)}) copy-start(pred[128,512]{0,1:T(8,128)(4,1)} %fusion.38) | copy-start | bytes 196612
  359.2 1.0 copy-start.8
Sparse Core Ops, SparseCore 0:
  11.0 147.4 all-gather.6
  246.2 136.6 all-gather.8
where the time goes:
time: 401 us; the launch traced here: 399 us
  blocking collectives  233 us (58%)
  local copies, waits for them, and re-layouts  44.6 us (11%)
  matrix products  32.8 us (8%)
  other arithmetic  26.6 us (7%)
  waiting for transfers between devices  24.6 us (6%)
  starting transfers between devices  21.3 us (5%)
  between operations  15.9 us (4%)
    all_gather x1, blocking collectives, shards(): lax.all_gather(value_weight, 'wide', axis=0, tiled=True)  109 us
    all_gather x1, blocking collectives, shards(): lax.all_gather(key_weight, 'wide', axis=0, tiled=True)  100 us
    ppermute x8, starting transfers between devices, from_partner(): return lax.ppermute(block, axis, route)  21.2 us
    unnamed x40, local copies, waits for them, and re-layouts  18.5 us
    ppermute x8, waiting for transfers between devices, from_partner(): return lax.ppermute(block, axis, route)  12.7 us
    all_gather x1, blocking collectives, shards(): whole = lax.all_gather(tokens_in, 'narrow', axis=1, tiled=True)  12.4 us
    dot_general x9, matrix products, step(): jnp.einsum('tgrk,gdk->tgrd', weights.astype(jnp.bfloat16), block_values,...  12.2 us
    dot_general x9, matrix products, step(): jnp.einsum('tgrd,gdk->tgrk', queries, block_keys, preferred_element_type=...  12 us
  transfers between devices with their start and end apart: 10, of which 4 were waited for; matrix products, arithmetic and copies ran while one was open for 23% of the time, Pallas kernels for 0%

commit v1 on v0

--- a/solution.py
+++ b/solution.py
@@ -109,7 +109,14 @@
     append_slot,
     shard_owner,
 ):
-    whole = lax.all_gather(tokens_in, "narrow", axis=1, tiled=True)
+    ring = [tokens_in]
+    for hop in range(3):
+        ring.append(lax.ppermute(ring[-1], "narrow", [(dev, (dev + 1) % 4) for dev in range(4)]))
+    whole = jnp.roll(
+        jnp.concatenate(ring[::-1], axis=1),
+        (lax.axis_index("narrow") + 1) * ring[0].shape[1],
+        axis=1,
+    )
     normed = rms_normed(whole, norm_gain)
     tok_rows = whole.shape[0]
     query_width = query_weight.shape[1]

time: 401 us -> 401 us (level)
  blocking collectives: 233 us -> 217 us
  starting transfers between devices: 21.3 us -> 33.3 us
  local copies, waits for them, and re-layouts: 44.6 us -> 55.9 us
  waiting for transfers between devices: 24.6 us -> 16.4 us
    all_gather x1 -> x0, blocking collectives: 12.4 us -> none  [shards(): whole = lax.all_gather(tokens_in, 'narrow', axis=1, tiled=True)]
    all_gather x1, waiting for transfers between devices: 11.2 us -> 0.01 us  [shards(): lax.all_gather(out_weight, 'wide', axis=0, tiled=True)]
    ppermute x0 -> x3, starting transfers between devices: none -> 10.2 us  [shards(): lax.ppermute(ring[-1], 'narrow', [(dev, (dev + 1) % 4) for dev in range(4)])]
    while x8 -> x40, local copies, waits for them, and re-layouts: 0.02 us -> 9.69 us
    all_gather x1, blocking collectives: 109 us -> 105 us  [shards(): lax.all_gather(value_weight, 'wide', axis=0, tiled=True)]
    unnamed x40 -> x61, local copies, waits for them, and re-layouts: 18.5 us -> 21.8 us
  transfers between devices with their start and end apart: 10 -> 13, of which waited for: 4 -> 3; matrix products, arithmetic and copies ran while one was open for 23% -> 24% of each run, Pallas kernels for 0% -> 0%
where the time goes in v1:
time: 401 us; the launch traced here: 398 us
  blocking collectives  217 us (54%)
  local copies, waits for them, and re-layouts  55.9 us (14%)
  starting transfers between devices  33.3 us (8%)
  matrix products  31 us (8%)
  other arithmetic  27.8 us (7%)
  waiting for transfers between devices  16.4 us (4%)
  between operations  16 us (4%)
    all_gather x1, blocking collectives, shards(): lax.all_gather(value_weight, 'wide', axis=0, tiled=True)  105 us
    all_gather x1, blocking collectives, shards(): lax.all_gather(key_weight, 'wide', axis=0, tiled=True)  100 us
    ppermute x8, starting transfers between devices, from_partner(): return lax.ppermute(block, axis, route)  23.1 us
    unnamed x61, local copies, waits for them, and re-layouts  21.8 us
    ppermute x8, waiting for transfers between devices, from_partner(): return lax.ppermute(block, axis, route)  14.3 us
    dot_general x9, matrix products, step(): jnp.einsum('tgrk,gdk->tgrd', weights.astype(jnp.bfloat16), block_values,...  12.2 us
    dot_general x9, matrix products, step(): jnp.einsum('tgrd,gdk->tgrk', queries, block_keys, preferred_element_type=...  12 us
    all_gather x1, blocking collectives, shards(): all_heads = lax.all_gather(attended, 'narrow', axis=1, tiled=True)  11.9 us
  transfers between devices with their start and end apart: 13, of which 3 were waited for; matrix products, arithmetic and copies ran while one was open for 24% of the time, Pallas kernels for 0%

profile of v1, /device:TPU:1, one launch (start us, length us, event | category | flops | bytes accessed | tf_op | source)
XLA Modules:
  0.0 397.8 jit_solution(2868213210408274112)
XLA Ops:
  8.0 4.0 %collective-permute-start.2 = (bf16[128,640]{1,0:T(8,128)(2,1)}, bf16[128,640]{1,0:T(8,128)(2,1)}, u32[]{:S(2)}, u32[]{:S(2)}) collective-permute-start(bf16[128,640]{1,0:T(8,128)(2,1)} %param.15), channel_id=1, source_target_pairs={{0,1},{1,2},{2,3},{3,0},{4,5},{5,6},{6,7},{7,4},{8,9},{9,10},{10,1... | collective-permute-start | bytes 491528 | tf_op jit(solution)/shard_map/ppermute | solution.py:114
  12.0 6.7 %collective-permute-start.5 = (bf16[160,1024]{1,0:T(8,128)(2,1)}, bf16[160,1024]{1,0:T(8,128)(2,1)}, u32[]{:S(2)}, u32[]{:S(2)}) collective-permute-start(bf16[160,1024]{1,0:T(8,128)(2,1)} %param.22), channel_id=1, source_target_pairs={{0,4},{4,0},{8,12},{12,8},{16,20},{20,16},{24,28},{28,24},{32,36},... | collective-permute-start | bytes 983048 | tf_op jit(solution)/shard_map/ppermute | solution.py:23
  18.7 1.9 collective-permute-start
  23.3 104.8 %all-gather.2 = bf16[128,20,160]{2,1,0:T(8,128)(2,1)S(1)} all-gather(bf16[1,20,160]{2,1,0:T(8,128)(2,1)} %bitcast.135), channel_id=1, replica_groups=mesh['wide'=128,'narrow'=4] {'wide'}, dimensions={0}, use_global_device_ids=true | all-gather | bytes 825600 | tf_op jit(solution)/shard_map/all_gather | solution.py:140
  128.1 100.1 %all-gather.1 = bf16[128,20,160]{2,1,0:T(8,128)(2,1)S(1)} all-gather(bf16[1,20,160]{2,1,0:T(8,128)(2,1)S(1)} %bitcast.136), channel_id=1, replica_groups=mesh['wide'=128,'narrow'=4] {'wide'}, dimensions={0}, use_global_device_ids=true | all-gather | bytes 825600 | tf_op jit(solution)/shard_map/all_gather | solution.py:135
  230.9 2.5 broadcast_compare_fusion
  235.4 3.2 collective-permute-start.3
  240.9 2.0 copy.39
  242.9 1.5 reshape.269
  245.0 2.5 add_select_fusion
  247.5 2.9 collective-permute-start.4
  252.6 2.1 collective-permute-start.1
  261.5 3.3 collective-permute-start.9
  265.6 1.9 collective-permute-start.7
  268.5 1.9 collective-permute-start.6
  270.5 3.4 collective-permute-start.10
  273.9 1.9 collective-permute-start.8
  275.8 13.5 %collective-permute-done.10 = bf16[256,160]{0,1:T(8,128)(2,1)S(1)} collective-permute-done((bf16[256,160]{0,1:T(8,128)(2,1)S(1)}, bf16[256,160]{0,1:T(8,128)(2,1)S(1)}, u32[]{:S(2)}, u32[]{:S(2)}) %collective-permute-start.10) | collective-permute-done | bytes 81952 | tf_op jit(solution)/shard_map/ppermute | solution.py:23
  291.2 4.9 %gather_fusion.1 = bf16[1024,160]{1,0:T(8,128)(2,1)} fusion(bf16[160,512]{0,1:T(8,128)(2,1)S(1)} %copy.40, s32[1024]{0:T(1024)S(1)} %copy-done.13), kind=kCustom, calls=%fused_computation.1.clone | custom fusion | bytes 659456 | tf_op jit(solution)/shard_map/jit(_take)/gather | solution.py:213
  296.1 4.9 %gather_fusion = bf16[1024,160]{1,0:T(8,128)(2,1)} fusion(bf16[160,512]{0,1:T(8,128)(2,1)S(1)} %copy.38, s32[1024]{0:T(1024)S(1)} %copy-done.13), kind=kCustom, calls=%fused_computation.clone | custom fusion | bytes 659456 | tf_op jit(solution)/shard_map/jit(_take)/gather | solution.py:212
  301.1 2.6 bitcast_select_fusion.2
  303.6 1.9 copy.42
  311.6 4.6 %reshape.265 = bf16[2560,640]{1,0:T(8,128)(2,1)S(1)} reshape(bf16[128,20,640]{2,1,0:T(8,128)(2,1)} %all-gather.7.cloned.1.call-done) | data formatting | bytes 6553600
  316.3 2.8 fusion.64
  319.2 50.6 %while.5 = (s32[]{:T(128)}, f32[128,2,4,80]{0,3,2,1:T(8,128)}, f32[128,2,4]{0,2,1:T(4,128)S(1)}, f32[128,2,4]{0,2,1:T(4,128)S(1)}, pred[4096]{0:T(1024)(128)(4,1...) while((s32[]{:T(128)}, f32[128,2,4,80]{0,3,2,1:T(8,128)}, ...), condition=%wide.region_4.5_spmd.clone, body=%wide.region_1.4_spmd.clone.sunk | while | flops 174118016 | bytes 10396435 | solution.py:96
  323.3 1.5 fusion.89
  329.6 1.5 fusion.89
  355.0 1.5 fusion.89
  367.6 1.5 fusion.89
  371.9 11.9 %all_gather.18 = bf16[128,2560]{0,1:T(8,128)(2,1)} all-gather(bf16[128,640]{0,1:T(8,128)(2,1)S(1)} %bitcast.129), channel_id=1, replica_groups=mesh['wide'=128,'narrow'=4] {'narrow'}, dimensions={1}, use_global_device_ids=true | all-gather | bytes 819200 | tf_op jit(solution)/shard_map/all_gather | solution.py:202
  383.8 4.6 %reshape.271 = bf16[2560,640]{1,0:T(8,128)(2,1)S(1)} reshape(bf16[128,20,640]{2,1,0:T(8,128)(2,1)} %all-gather.9.cloned.1.call-done) | data formatting | bytes 6553600
  388.5 2.5 convolution_convert_fusion
  (225 shorter events, 74.5 us)
Async XLA Ops:
  7.2 120.9 %copy-start.14 = (bf16[20,160]{1,0:T(8,128)(2,1)S(1)}, bf16[20,160]{1,0:T(8,128)(2,1)}, u32[]{:S(2)}) copy-start(bf16[20,160]{1,0:T(8,128)(2,1)} %param.18) | copy-start | bytes 19204
  7.2 304.4 %all-gather.7.cloned.1.call-start = ((), (), s32[]{:S(2)}) async-start(), calls=%async_computation | async-start | bytes 3962880 | tf_op jit(solution)/shard_map/all_gather | solution.py:130
  7.9 375.9 %all-gather.9.cloned.1.call-start = ((), (), s32[]{:S(2)}) async-start(), calls=%async_computation.1 | async-start | bytes 3962880 | tf_op jit(solution)/shard_map/all_gather | solution.py:206
  8.0 227.4 %collective-permute-start.2 = (bf16[128,640]{1,0:T(8,128)(2,1)}, bf16[128,640]{1,0:T(8,128)(2,1)}, u32[]{:S(2)}, u32[]{:S(2)}) collective-permute-start(bf16[128,640]{1,0:T(8,128)(2,1)} %param.15), channel_id=1, source_target_pairs={{0,1},{1,2},{2,3},{3,0},{4,5},{5,6},{6,7},{7,4},{8,9},{9,10},{10,1... | collective-permute-start | bytes 491528 | tf_op jit(solution)/shard_map/ppermute | solution.py:114
  12.0 238.4 %collective-permute-start.5 = (bf16[160,1024]{1,0:T(8,128)(2,1)}, bf16[160,1024]{1,0:T(8,128)(2,1)}, u32[]{:S(2)}, u32[]{:S(2)}) collective-permute-start(bf16[160,1024]{1,0:T(8,128)(2,1)} %param.22), channel_id=1, source_target_pairs={{0,4},{4,0},{8,12},{12,8},{16,20},{20,16},{24,28},{28,24},{32,36},... | collective-permute-start | bytes 983048 | tf_op jit(solution)/shard_map/ppermute | solution.py:23
  18.7 231.8 %collective-permute-start = (bf16[160,1024]{1,0:T(8,128)(2,1)}, bf16[160,1024]{1,0:T(8,128)(2,1)}, u32[]{:S(2)}, u32[]{:S(2)}) collective-permute-start(bf16[160,1024]{1,0:T(8,128)(2,1)} %param.21), channel_id=1, source_target_pairs={{0,4},{4,0},{8,12},{12,8},{16,20},{20,16},{24,28},{28,24},{32,36},... | collective-permute-start | bytes 983048 | tf_op jit(solution)/shard_map/ppermute | solution.py:23
  23.3 204.8 %copy-start.20 = (s32[32]{0:T(128)S(1)}, s32[32]{0:T(128)}, u32[]{:S(2)}) copy-start(s32[32]{0:T(128)} %param.24) | copy-start | bytes 388
  23.3 205.5 %copy-start.21 = (s32[32]{0:T(128)S(1)}, s32[32]{0:T(128)}, u32[]{:S(2)}) copy-start(s32[32]{0:T(128)} %param.25) | copy-start | bytes 388
  23.3 216.6 %copy-start.4 = (bf16[160,1024]{1,0:T(8,128)(2,1)S(1)}, bf16[160,1024]{1,0:T(8,128)(2,1)}, u32[]{:S(2)}) copy-start(bf16[160,1024]{1,0:T(8,128)(2,1)} %param.22) | copy-start | bytes 983044
  235.4 12.2 %collective-permute-start.3 = (bf16[128,640]{1,0:T(8,128)(2,1)}, bf16[128,640]{1,0:T(8,128)(2,1)}, u32[]{:S(2)}, u32[]{:S(2)}) collective-permute-start(bf16[128,640]{1,0:T(8,128)(2,1)} %collective-permute-done.2), channel_id=1, source_target_pairs={{0,1},{1,2},{2,3},{3,0},{4,5},{5,6},{6,7},{7,4},{8,9},{9,10},{10,1... | collective-permute-start | bytes 491528 | tf_op jit(solution)/shard_map/ppermute | solution.py:114
  247.5 8.6 %collective-permute-start.4 = (bf16[128,640]{1,0:T(8,128)(2,1)}, bf16[128,640]{1,0:T(8,128)(2,1)S(1)}, u32[]{:S(2)}, u32[]{:S(2)}) collective-permute-start(bf16[128,640]{1,0:T(8,128)(2,1)} %collective-permute-done.3), channel_id=1, source_target_pairs={{0,1},{1,2},{2,3},{3,0},{4,5},{5,6},{6,7},{7,4},{8,9},{9,10},{10,1... | collective-permute-start | bytes 491528 | tf_op jit(solution)/shard_map/ppermute | solution.py:114
  251.7 6.5 %copy-start.5 = (bf16[128,640]{1,0:T(8,128)(2,1)S(1)}, bf16[128,640]{1,0:T(8,128)(2,1)}, u32[]{:S(2)}) copy-start(bf16[128,640]{1,0:T(8,128)(2,1)} %param.15) | copy-start | bytes 491524
  252.6 53.9 %collective-permute-start.1 = (bf16[160,2048]{1,0:T(8,128)(2,1)}, bf16[160,2048]{1,0:T(8,128)(2,1)}, u32[]{:S(2)}, u32[]{:S(2)}) collective-permute-start(bf16[160,2048]{1,0:T(8,128)(2,1)} %pad_maximum_fusion.2), channel_id=1, source_target_pairs={{0,8},{8,0},{4,12},{12,4},{16,24},{24,16},{20,28},{28,20},{32,40},... | collective-permute-start | bytes 1966088 | tf_op jit(solution)/shard_map/ppermute | solution.py:23
  257.1 3.5 copy-start.1
  260.2 4.6 %copy-start = (bf16[128,5120]{1,0:T(8,128)(2,1)}, bf16[128,5120]{1,0:T(8,128)(2,1)S(1)}, u32[]{:S(2)}) copy-start(bf16[128,5120]{1,0:T(8,128)(2,1)S(1)} %constant_dynamic-update-slice_fusion) | copy-start | bytes 3932164
  260.6 5.0 %copy-start.16 = (f32[128]{0:T(128)}, f32[128]{0:T(128)S(1)}, u32[]{:S(2)}) copy-start(f32[128]{0:T(128)S(1)} %add_rsqrt_fusion) | copy-start | bytes 1540
  261.4 4.2 %copy-start.7 = (f32[128,40]{0,1:T(8,128)S(1)}, f32[128,40]{0,1:T(8,128)}, u32[]{:S(2)}) copy-start(f32[128,40]{0,1:T(8,128)} %get-tuple-element.305) | copy-start | bytes 61444
  261.4 4.2 %copy-start.9 = (f32[128,40]{0,1:T(8,128)S(1)}, f32[128,40]{0,1:T(8,128)}, u32[]{:S(2)}) copy-start(f32[128,40]{0,1:T(8,128)} %get-tuple-element.306) | copy-start | bytes 61444
  261.5 9.0 %collective-permute-start.9 = (bf16[128,160]{0,1:T(8,128)(2,1)S(1)}, bf16[128,160]{0,1:T(8,128)(2,1)S(1)}, u32[]{:S(2)}, u32[]{:S(2)}) collective-permute-start(bf16[128,160]{0,1:T(8,128)(2,1)S(1)} %convolution_convert_fusion.1), channel_id=1, source_target_pairs={{0,4},{4,0},{8,12},{12,8},{16,20},{20,16},{24,28},{28,24},{32,36},... | collective-permute-start | bytes 122888 | tf_op jit(solution)/shard_map/ppermute | solution.py:23
  265.6 4.8 %collective-permute-start.7 = (bf16[128,160]{0,1:T(8,128)(2,1)S(1)}, bf16[128,160]{0,1:T(8,128)(2,1)S(1)}, u32[]{:S(2)}, u32[]{:S(2)}) collective-permute-start(bf16[128,160]{0,1:T(8,128)(2,1)S(1)} %bitcast.127), channel_id=1, source_target_pairs={{0,4},{4,0},{8,12},{12,8},{16,20},{20,16},{24,28},{28,24},{32,36},... | collective-permute-start | bytes 122888 | tf_op jit(solution)/shard_map/ppermute | solution.py:23
  268.5 40.5 %collective-permute-start.6 = (bf16[160,2048]{1,0:T(8,128)(2,1)}, bf16[160,2048]{1,0:T(8,128)(2,1)}, u32[]{:S(2)}, u32[]{:S(2)}) collective-permute-start(bf16[160,2048]{1,0:T(8,128)(2,1)} %pad_maximum_fusion.3), channel_id=1, source_target_pairs={{0,8},{8,0},{4,12},{12,4},{16,24},{24,16},{20,28},{28,20},{32,40},... | collective-permute-start | bytes 1966088 | tf_op jit(solution)/shard_map/ppermute | solution.py:23
  270.5 18.8 %collective-permute-start.10 = (bf16[256,160]{0,1:T(8,128)(2,1)S(1)}, bf16[256,160]{0,1:T(8,128)(2,1)S(1)}, u32[]{:S(2)}, u32[]{:S(2)}) collective-permute-start(bf16[256,160]{0,1:T(8,128)(2,1)S(1)} %pad_maximum_fusion.8), channel_id=1, source_target_pairs={{0,8},{8,0},{4,12},{12,4},{16,24},{24,16},{20,28},{28,20},{32,40},... | collective-permute-start | bytes 245768 | tf_op jit(solution)/shard_map/ppermute | solution.py:23
  273.9 17.3 %copy-start.13 = (s32[1024]{0:T(1024)S(1)}, s32[1024]{0:T(1024)}, u32[]{:S(2)}) copy-start(s32[1024]{0:T(1024)} %fusion.54) | copy-start | bytes 12292
  273.9 17.0 %collective-permute-start.8 = (bf16[256,160]{0,1:T(8,128)(2,1)S(1)}, bf16[256,160]{0,1:T(8,128)(2,1)S(1)}, u32[]{:S(2)}, u32[]{:S(2)}) collective-permute-start(bf16[256,160]{0,1:T(8,128)(2,1)S(1)} %pad_maximum_fusion.7), channel_id=1, source_target_pairs={{0,8},{8,0},{4,12},{12,4},{16,24},{24,16},{20,28},{28,20},{32,40},... | collective-permute-start | bytes 245768 | tf_op jit(solution)/shard_map/ppermute | solution.py:23
  296.1 5.0 %copy-start.2 = (bf16[160,1024]{0,1:T(8,128)(2,1)S(1)}, bf16[160,1024]{0,1:T(8,128)(2,1)}, u32[]{:S(2)}) copy-start(bf16[160,1024]{0,1:T(8,128)(2,1)} %copy.41) | copy-start | bytes 983044
  296.1 5.0 %copy-start.3 = (bf16[160,1024]{0,1:T(8,128)(2,1)S(1)}, bf16[160,1024]{0,1:T(8,128)(2,1)}, u32[]{:S(2)}) copy-start(bf16[160,1024]{0,1:T(8,128)(2,1)} %copy.39) | copy-start | bytes 983044
  296.1 5.0 %copy-start.18 = (pred[1024]{0:T(1024)(128)(4,1)S(1)}, pred[1024]{0:T(1024)(128)(4,1)}, u32[]{:S(2)}) copy-start(pred[1024]{0:T(1024)(128)(4,1)} %get-tuple-element.313) | copy-start | bytes 3076
  296.1 5.0 %copy-start.19 = (pred[1024]{0:T(1024)(128)(4,1)S(1)}, pred[1024]{0:T(1024)(128)(4,1)}, u32[]{:S(2)}) copy-start(pred[1024]{0:T(1024)(128)(4,1)} %get-tuple-element.314) | copy-start | bytes 3076
  311.6 4.7 %copy-start.17 = (f32[128]{0:T(128)S(1)}, f32[128]{0:T(128)}, u32[]{:S(2)}) copy-start(f32[128]{0:T(128)} %copy-done.16) | copy-start | bytes 1540
  316.3 2.8 copy-start.8
  316.3 2.9 copy-start.12
  319.2 50.6 %copy-start.6 = (pred[128,512]{0,1:T(8,128)(4,1)S(1)}, pred[128,512]{0,1:T(8,128)(4,1)}, u32[]{:S(2)}) copy-start(pred[128,512]{0,1:T(8,128)(4,1)} %fusion.38) | copy-start | bytes 196612
  (20 other events, 20.0 us)
Sparse Core Ops, SparseCore 0:
  11.1 147.5 all-gather.6
  161.7 137.8 all-gather.8
